TPU v7x, 256 devices: a whole 4x4x8 slice. The times are simulated.
256 devices in a mesh: dp: 64 (over z, y, core), tensor: 4 (over x).
Axes of the slice: x: 4, y: 4, z: 8, core: 2. Of those that a mesh axis runs over, the one named last changes fastest.
Arguments:
- inputs: bfloat16 [45056, 1280], P('dp'), may hold values from -24 to 24
- targets: bfloat16 [45056, 1280], P('dp'), may hold values from -6 to 6
- w_in: bfloat16 [1280, 5120], P(None, 'tensor'), may hold values from -0.15625 to 0.15625
- w_out: bfloat16 [5120, 1280], P('tensor'), may hold values from -0.078125 to 0.078125
Outputs:
- merged_in: float32 [1280, 5120], P('dp', 'tensor')
- merged_out: float32 [1280, 5120], P('dp', 'tensor')
All inputs are finite; a program needn't handle non-finite values.
Results may differ from a plain program's by a relative error of at most 0.0033.
Values may be sent and summed in bfloat16 or wider, within the bound.
A program may use at most 128 MiB of HBM per device.

v0:
```python
import jax
import jax.numpy as jnp
from jax import lax
from jax.sharding import PartitionSpec as P

epsilon = 1e-06


def copy_for_each(x, axis):
    copies = jnp.broadcast_to(x, (lax.axis_size(axis), *x.shape))
    return lax.all_to_all(copies, axis, split_axis=0, concat_axis=0, tiled=True)


def taken_together(x, axis):
    everything = copy_for_each(x, axis)
    return jnp.sum(everything, axis=0)


def from_partner(value, axis, distance):
    mask = 2**distance
    pairs = [(source, source ^ mask) for source in range(lax.axis_size(axis))]
    return lax.ppermute(value, axis, pairs)


def cut_along(x, dim, count):
    before, after = (x.shape[:dim], x.shape[dim + 1 :])
    return jnp.moveaxis(x.reshape(*before, count, -1, *after), dim, 0)


def sum_at_owner(x, axis, dim):
    count = lax.axis_size(axis)
    tiles = lax.all_to_all(cut_along(x, dim, count), axis, 0, 0, tiled=True)
    return jnp.sum(tiles, axis=0)


def activate(values):
    return jax.nn.gelu(values, approximate=True)


def split_piece(piece, upper_flag):
    half = piece.shape[0] // 2
    keep = lax.dynamic_slice_in_dim(piece, upper_flag * half, half, 0)
    send = lax.dynamic_slice_in_dim(piece, (1 - upper_flag) * half, half, 0)
    return (keep, send)


def group_total(values, section, levels):
    summed = taken_together(values, "tensor")
    for offset in range(section + 1):
        summed = summed + from_partner(summed, "dp", levels - 1 - offset)
    return summed


def combine(own, incoming, upper_flag, section, levels):
    product = jnp.sum(own[0] * incoming[0]) + jnp.sum(own[1] * incoming[1])
    norm_own = jnp.sum(own[0] * own[0]) + jnp.sum(own[1] * own[1])
    norm_incoming = jnp.sum(incoming[0] * incoming[0]) + jnp.sum(incoming[1] * incoming[1])
    is_upper = upper_flag == 1
    norm_low = jnp.where(is_upper, norm_incoming, norm_own)
    norm_high = jnp.where(is_upper, norm_own, norm_incoming)
    totals = group_total(jnp.stack([product, norm_low, norm_high]), section, levels)
    coef_low = 1.0 - totals[0] / (2.0 * (totals[1] + epsilon))
    coef_high = 1.0 - totals[0] / (2.0 * (totals[2] + epsilon))
    coef_own = jnp.where(is_upper, coef_high, coef_low)
    coef_incoming = jnp.where(is_upper, coef_low, coef_high)
    return (
        coef_own * own[0] + coef_incoming * incoming[0],
        coef_own * own[1] + coef_incoming * incoming[1],
    )


def on_device(inputs, targets, w_in, w_out):
    row_count = inputs.shape[0]
    preact = jnp.dot(inputs, w_in, preferred_element_type=jnp.float32)
    hidden = activate(preact).astype(jnp.bfloat16)
    partial_out = jnp.dot(hidden, w_out, preferred_element_type=jnp.float32)
    share = row_count // lax.axis_size("tensor")
    mine = sum_at_owner(partial_out, "tensor", 0)
    target_rows = lax.dynamic_slice_in_dim(targets, lax.axis_index("tensor") * share, share, 0)
    error_share = ((mine - target_rows.astype(jnp.float32)) / row_count).astype(jnp.bfloat16)
    error = lax.all_gather(error_share, "tensor", axis=0, tiled=True)
    back = jnp.dot(error, w_out.T, preferred_element_type=jnp.float32)
    _, pullback = jax.vjp(activate, preact)
    dpre = pullback(back)[0].astype(jnp.bfloat16)
    contract_rows = (((0,), (0,)), ((), ()))
    second = lax.dot_general(error, hidden, contract_rows, preferred_element_type=jnp.float32)
    levels = lax.axis_size("dp").bit_length() - 1
    position = lax.axis_index("dp")

    def flag_of(section):
        return position >> levels - 1 - section & 1

    upper_flag = flag_of(0)
    keep_second, send_second = split_piece(second, upper_flag)
    got_second = from_partner(send_second.astype(jnp.bfloat16), "dp", levels - 1).astype(
        send_second.dtype
    )
    first = lax.dot_general(inputs, dpre, contract_rows, preferred_element_type=jnp.float32)
    keep_first, send_first = split_piece(first, upper_flag)
    got_first = from_partner(send_first, "dp", levels - 1)
    pieces = combine((keep_first, keep_second), (got_first, got_second), upper_flag, 0, levels)
    begin = 1
    for section in range(begin, levels):
        upper_flag = flag_of(section)
        keep_first, send_first = split_piece(pieces[0], upper_flag)
        keep_second, send_second = split_piece(pieces[1], upper_flag)
        got_first, got_second = from_partner((send_first, send_second), "dp", levels - 1 - section)
        pieces = combine(
            (keep_first, keep_second), (got_first, got_second), upper_flag, section, levels
        )
    return (pieces[0], pieces[1])


def solution(mesh):
    placed = (P("dp", None), P("dp", None), P(None, "tensor"), P("tensor", None))
    return jax.shard_map(
        on_device,
        mesh=mesh,
        in_specs=placed,
        out_specs=(P("dp", "tensor"), P("dp", "tensor")),
        check_vma=False,
    )
```

profile of v0, /device:TPU:1, one launch (start us, length us, event | category | flops | bytes accessed | tf_op | source)
XLA Modules:
  0.0 777.2 jit_solution(13977184654321985071)
XLA Ops:
  7.2 5.1 fusion.31
  22.2 40.5 %all-to-all-done = f32[4,176,1280]{2,1,0:T(8,128)} async-done(((f32[4,176,1280]{2,1,0:T(8,128)}), f32[4,176,1280]{2,1,0:T(8,128)}, u32[]{:S(2)}, u32[]{:S(2)}) %all-to-all-start) | async-done | bytes 3604512 | tf_op jit(solution)/shard_map/all_to_all | solution.py:32
  68.2 35.0 %all-gather.2.cloned.1.call-done = bf16[704,1280]{1,0:T(8,128)(2,1)} async-done(((bf16[176,1280]{1,0:T(8,128)(2,1)}), bf16[704,1280]{1,0:T(8,128)(2,1)}) %all-gather.2.cloned.1.call-update) | async-done | bytes 1802256 | tf_op jit(solution)/shard_map/all_gather | solution.py:81
  103.2 12.3 %fusion.13 = f32[1280,1280]{0,1:T(8,128)} fusion(bf16[704,1280]{1,0:T(8,128)(2,1)} %param.4, f32[704,1280]{1,0:T(8,128)} %copy-done.20, bf16[704,1280]{1,0:T(8,128)(2,1)} %all-gather.2.cloned.1.call-done, bf16[1280,1280]{1,0:T(8,128)(2,1)S(1)} %copy-done), kind=kOutput, calls=%fused_computation.26 | convolution fusion | flops 4631756800 | bytes 17039360 | tf_op jit(solution)/shard_map/dot_general | solution.py:98
  119.5 5.8 collective-permute-start
  132.3 205.7 %collective-permute-done.1 = bf16[640,1280]{1,0:T(8,128)(2,1)} collective-permute-done((bf16[640,1280]{1,0:T(8,128)(2,1)}, bf16[640,1280]{1,0:T(8,128)(2,1)}, u32[]{:S(2)}, u32[]{:S(2)}) %collective-permute-start.1) | collective-permute-done | bytes 1638432 | tf_op jit(solution)/shard_map/ppermute | solution.py:22
  350.4 6.6 all_to_all.41
  357.0 5.8 collective-permute-start.2
  367.2 5.1 fusion.9
  377.4 104.3 %collective-permute-done.4 = f32[320,1280]{1,0:T(8,128)} collective-permute-done((f32[320,1280]{1,0:T(8,128)}, f32[320,1280]{1,0:T(8,128)}, u32[]{:S(2)}, u32[]{:S(2)}) %collective-permute-start.4) | collective-permute-done | bytes 1638432 | tf_op jit(solution)/shard_map/ppermute | solution.py:22
  484.6 32.1 %collective-permute-done.3 = f32[320,1280]{1,0:T(8,128)} collective-permute-done((f32[320,1280]{1,0:T(8,128)}, f32[320,1280]{1,0:T(8,128)}, u32[]{:S(2)}, u32[]{:S(2)}) %collective-permute-start.3) | collective-permute-done | bytes 1638432 | tf_op jit(solution)/shard_map/ppermute | solution.py:22
  523.0 6.5 all_to_all.42
  529.5 5.1 collective-permute-start.5
  550.3 11.5 %collective-permute-done.8 = f32[160,1280]{1,0:T(8,128)} collective-permute-done((f32[160,1280]{1,0:T(8,128)}, f32[160,1280]{1,0:T(8,128)}, u32[]{:S(2)}, u32[]{:S(2)}) %collective-permute-start.8) | collective-permute-done | bytes 819232 | tf_op jit(solution)/shard_map/ppermute | solution.py:22
  564.1 15.3 %collective-permute-done.7 = f32[160,1280]{1,0:T(8,128)} collective-permute-done((f32[160,1280]{1,0:T(8,128)}, f32[160,1280]{1,0:T(8,128)}, u32[]{:S(2)}, u32[]{:S(2)}) %collective-permute-start.7) | collective-permute-done | bytes 819232 | tf_op jit(solution)/shard_map/ppermute | solution.py:22
  585.4 6.5 all_to_all.43
  591.9 5.1 collective-permute-start.9
  626.8 6.5 all_to_all.44
  633.3 5.1 collective-permute-start.14
  670.0 6.5 all_to_all.45
  676.4 5.1 collective-permute-start.20
  699.4 24.5 %collective-permute-start.26 = (f32[20,1280]{1,0:T(8,128)S(1)}, f32[20,1280]{1,0:T(8,128)S(1)}, u32[]{:S(2)}, u32[]{:S(2)}) collective-permute-start(f32[20,1280]{1,0:T(8,128)S(1)} %constant_dynamic-slice_fusion), channel_id=1, source_target_pairs={{0,4},{4,0},{8,12},{12,8},{16,20},{20,16},{24,28},{28,24},{32,36},... | collective-permute-start | bytes 307208 | tf_op jit(solution)/shard_map/ppermute | solution.py:22
  731.0 6.5 all_to_all.46
  756.0 7.0 collective-permute-start.32
  (183 shorter events, 155.5 us)
Async XLA Ops:
  17.4 45.3 %all-to-all-start = ((f32[4,176,1280]{2,1,0:T(8,128)}), f32[4,176,1280]{2,1,0:T(8,128)}, u32[]{:S(2)}, u32[]{:S(2)}) async-start(f32[4,176,1280]{2,1,0:T(8,128)} %bitcast.50), calls=%async_computation | async-start | bytes 7208960 | tf_op jit(solution)/shard_map/all_to_all | solution.py:32
  22.2 81.0 %all-gather.2.cloned.1.call-start = ((), (), s32[]{:S(2)}) async-start(), calls=%async_computation.7 | async-start | bytes 2252800 | tf_op jit(solution)/shard_map/all_gather | solution.py:81
  119.5 222.4 %collective-permute-start = (f32[640,1280]{1,0:T(8,128)}, f32[640,1280]{1,0:T(8,128)S(1)}, u32[]{:S(2)}, u32[]{:S(2)}) collective-permute-start(f32[640,1280]{1,0:T(8,128)} %dynamic-slice_bitcast_fusion), channel_id=1, source_target_pairs={{0,128},{4,132},{8,136},{12,140},{16,144},{20,148},{24,152},{28,15... | collective-permute-start | bytes 9830408 | tf_op jit(solution)/shard_map/ppermute | solution.py:22
  132.2 205.7 %collective-permute-start.1 = (bf16[640,1280]{1,0:T(8,128)(2,1)}, bf16[640,1280]{1,0:T(8,128)(2,1)}, u32[]{:S(2)}, u32[]{:S(2)}) collective-permute-start(bf16[640,1280]{1,0:T(8,128)(2,1)} %dynamic-slice_convert_fusion), channel_id=1, source_target_pairs={{0,128},{4,132},{8,136},{12,140},{16,144},{20,148},{24,152},{28,15... | collective-permute-start | bytes 4915208 | tf_op jit(solution)/shard_map/ppermute | solution.py:22
  357.0 6.8 collective-permute-start.2
  373.7 107.9 %collective-permute-start.4 = (f32[320,1280]{1,0:T(8,128)}, f32[320,1280]{1,0:T(8,128)}, u32[]{:S(2)}, u32[]{:S(2)}) collective-permute-start(f32[320,1280]{1,0:T(8,128)} %constant_dynamic-slice_fusion.8), channel_id=1, source_target_pairs={{0,64},{4,68},{8,72},{12,76},{16,80},{20,84},{24,88},{28,92},{32,9... | collective-permute-start | bytes 4915208 | tf_op jit(solution)/shard_map/ppermute | solution.py:22
  375.0 141.7 %collective-permute-start.3 = (f32[320,1280]{1,0:T(8,128)}, f32[320,1280]{1,0:T(8,128)}, u32[]{:S(2)}, u32[]{:S(2)}) collective-permute-start(f32[320,1280]{1,0:T(8,128)} %constant_dynamic-slice_fusion.9), channel_id=1, source_target_pairs={{0,64},{4,68},{8,72},{12,76},{16,80},{20,84},{24,88},{28,92},{32,9... | collective-permute-start | bytes 4915208 | tf_op jit(solution)/shard_map/ppermute | solution.py:22
  529.5 6.4 collective-permute-start.5
  545.6 16.2 %collective-permute-start.8 = (f32[160,1280]{1,0:T(8,128)}, f32[160,1280]{1,0:T(8,128)}, u32[]{:S(2)}, u32[]{:S(2)}) collective-permute-start(f32[160,1280]{1,0:T(8,128)} %constant_dynamic-slice_fusion.6), channel_id=1, source_target_pairs={{0,32},{4,36},{8,40},{12,44},{16,48},{20,52},{24,56},{28,60},{32,0... | collective-permute-start | bytes 2457608 | tf_op jit(solution)/shard_map/ppermute | solution.py:22
  548.7 30.7 %collective-permute-start.7 = (f32[160,1280]{1,0:T(8,128)}, f32[160,1280]{1,0:T(8,128)}, u32[]{:S(2)}, u32[]{:S(2)}) collective-permute-start(f32[160,1280]{1,0:T(8,128)} %constant_dynamic-slice_fusion.7), channel_id=1, source_target_pairs={{0,32},{4,36},{8,40},{12,44},{16,48},{20,52},{24,56},{28,60},{32,0... | collective-permute-start | bytes 2457608 | tf_op jit(solution)/shard_map/ppermute | solution.py:22
  591.9 6.4 collective-permute-start.9
  598.3 3.3 collective-permute-start.10
  609.1 8.5 %collective-permute-start.13 = (f32[80,1280]{1,0:T(8,128)}, f32[80,1280]{1,0:T(8,128)S(1)}, u32[]{:S(2)}, u32[]{:S(2)}) collective-permute-start(f32[80,1280]{1,0:T(8,128)} %constant_dynamic-slice_fusion.4), channel_id=1, source_target_pairs={{0,16},{4,20},{8,24},{12,28},{16,0},{20,4},{24,8},{28,12},{32,48},... | collective-permute-start | bytes 1228808 | tf_op jit(solution)/shard_map/ppermute | solution.py:22
  613.2 8.9 %collective-permute-start.12 = (f32[80,1280]{1,0:T(8,128)S(1)}, f32[80,1280]{1,0:T(8,128)S(1)}, u32[]{:S(2)}, u32[]{:S(2)}) collective-permute-start(f32[80,1280]{1,0:T(8,128)S(1)} %constant_dynamic-slice_fusion.5), channel_id=1, source_target_pairs={{0,16},{4,20},{8,24},{12,28},{16,0},{20,4},{24,8},{28,12},{32,48},... | collective-permute-start | bytes 1228808 | tf_op jit(solution)/shard_map/ppermute | solution.py:22
  633.3 6.4 collective-permute-start.14
  645.4 3.9 collective-permute-start.17
  655.4 4.8 collective-permute-start.19
  659.2 5.1 collective-permute-start.18
  676.4 6.4 collective-permute-start.20
  688.6 3.9 collective-permute-start.23
  699.4 25.9 %collective-permute-start.26 = (f32[20,1280]{1,0:T(8,128)S(1)}, f32[20,1280]{1,0:T(8,128)S(1)}, u32[]{:S(2)}, u32[]{:S(2)}) collective-permute-start(f32[20,1280]{1,0:T(8,128)S(1)} %constant_dynamic-slice_fusion), channel_id=1, source_target_pairs={{0,4},{4,0},{8,12},{12,8},{16,20},{20,16},{24,28},{28,24},{32,36},... | collective-permute-start | bytes 307208 | tf_op jit(solution)/shard_map/ppermute | solution.py:22
  737.5 6.4 collective-permute-start.27
  749.7 3.9 collective-permute-start.30
  756.0 7.9 %collective-permute-start.32 = (f32[3]{0:T(128)S(1)}, f32[3]{0:T(128)S(1)}, u32[]{:S(2)}, u32[]{:S(2)}) collective-permute-start(f32[3]{0:T(128)S(1)} %add.333), channel_id=1, source_target_pairs={{0,4},{4,0},{8,12},{12,8},{16,20},{20,16},{24,28},{28,24},{32,36},... | collective-permute-start | bytes 44 | tf_op jit(solution)/shard_map/ppermute | solution.py:22
  (33 other events, 433.9 us)
Sparse Core Ops, SparseCore 0:
  68.3 34.8 all-gather.1
where the time goes:
time: 787 us; the launch traced here: 777 us
  waiting for transfers between devices  497 us (63%)
  starting transfers between devices  91.7 us (12%)
  between operations  52.5 us (7%)
  other arithmetic  51.3 us (7%)
  blocking collectives  38.9 us (5%)
  matrix products  25.4 us (3%)
  local copies, waits for them, and re-layouts  20.9 us (3%)
    ppermute x33, waiting for transfers between devices, from_partner(): return lax.ppermute(value, axis, pairs)  421 us
    ppermute x33, starting transfers between devices, from_partner(): return lax.ppermute(value, axis, pairs)  86.9 us
    all_to_all x1, waiting for transfers between devices, sum_at_owner(): tiles = lax.all_to_all(cut_along(x, dim, count), axis, 0, 0, tiled=True)  40.5 us
    all_to_all x6, blocking collectives, copy_for_each(): return lax.all_to_all(copies, axis, split_axis=0, concat_axis=0, tiled=True)  38.9 us
    all_gather x1, waiting for transfers between devices, on_device(): error = lax.all_gather(error_share, 'tensor', axis=0, tiled=True)  35 us
    reduce_sum x12, other arithmetic, combine(): product = jnp.sum(own[0] * incoming[0]) + jnp.sum(own[1] * incoming[1])  26.1 us
  transfers between devices with their start and end apart: 35, of which 33 were waited for; matrix products, arithmetic and copies ran while one was open for 3% of the time, Pallas kernels for 0%

commit v1 on v0

v1 whole, which is shorter than its diff:
```python
import functools
import math

import jax
import jax.numpy as jnp
from jax import lax
from jax.experimental import pallas as pl
from jax.experimental.pallas import tpu as pltpu
from jax.sharding import PartitionSpec as P

F32, BF16 = jnp.float32, jnp.bfloat16
EPSILON = 1e-06
GELU_A = math.sqrt(2.0 / math.pi)
GELU_B = 0.044715
MESH = pl.DeviceIdType.MESH
BY_ROWS = (((1,), (1,)), ((), ()))


def tile_of(n):
    return 256 if n % 256 == 0 else n


def block(start, size, step):
    return pl.ds(pl.multiple_of(start, step), size)


def fold(v):
    rows, columns = v.shape
    t = v[0:8]
    for i in range(8, rows, 8):
        t = t + v[i : i + 8]
    s = t[:, :128]
    for j in range(128, columns, 128):
        s = s + t[:, j : j + 128]
    return s


def fold_row(v):
    t = jnp.sum(v, axis=0, keepdims=True)
    s = t[:, :128]
    for j in range(128, v.shape[1], 128):
        s = s + t[:, j : j + 128]
    return s


def pairs_of(n):
    return [(i, j) for i in range(n) for j in range(i, n)]


def tree_weights(gram, n):
    if n == 1:
        return [None]
    half = n // 2

    def at(i, j):
        return gram[(min(i, j), max(i, j))]

    low, high = [], []
    for j in range(half):
        product = at(j, j + half)
        low.append(1.0 - product / (2.0 * (at(j, j) + EPSILON)))
        high.append(1.0 - product / (2.0 * (at(j + half, j + half) + EPSILON)))
    if half == 1:
        return low + high
    merged = {}
    for j, k in pairs_of(half):
        merged[(j, k)] = (
            low[j] * low[k] * at(j, k)
            + low[j] * high[k] * at(j, k + half)
            + high[j] * low[k] * at(j + half, k)
            + high[j] * high[k] * at(j + half, k + half)
        )
    outer = tree_weights(merged, half)
    return [outer[j] * low[j] for j in range(half)] + [outer[j] * high[j] for j in range(half)]


def scratch_of(n_x, n_y, rows, width, hidden):
    n_z = 2 * n_y
    quarter = rows // n_x
    half, part, own = width // 2, width // (2 * n_y), width // (2 * n_y * n_z)
    stat_y = -(-len(pairs_of(n_y)) // 8) * 8
    stat_z = -(-len(pairs_of(n_z)) // 8) * 8
    group = 2 * n_x
    dma = pltpu.SemaphoreType.DMA
    return {
        "w_in": pltpu.VMEM((width, hidden), BF16),
        "w_out": pltpu.VMEM((hidden, width), BF16),
        "x": pltpu.VMEM((rows, width), BF16),
        "target": pltpu.VMEM((quarter, width), BF16),
        "order": pltpu.VMEM((width, width), BF16),
        "x_t": pltpu.VMEM((width, rows), BF16),
        "err_t": pltpu.VMEM((width, rows), BF16),
        "hid": pltpu.VMEM((rows, hidden), BF16),
        "slope": pltpu.VMEM((rows, hidden), F32),
        "out_own": pltpu.VMEM((quarter, width), F32),
        "out_send": pltpu.VMEM((n_x - 1, quarter, width), BF16),
        "out_recv": pltpu.VMEM((n_x - 1, quarter, width), BF16),
        "err": pltpu.VMEM((rows, width), BF16),
        "dpre": pltpu.VMEM((rows, hidden), BF16),
        "keep": pltpu.VMEM((2, half, hidden), F32),
        "send": pltpu.VMEM((2, half, hidden), BF16),
        "recv": pltpu.VMEM((2, half, hidden), BF16),
        "node": pltpu.VMEM((2, half, hidden), BF16),
        "y_recv": pltpu.VMEM((n_y, 2, part, hidden), BF16),
        "y_merged": pltpu.VMEM((2, part, hidden), F32),
        "z_send": pltpu.VMEM((n_z, 2, own, hidden), BF16),
        "z_recv": pltpu.VMEM((n_z, 2, own, hidden), BF16),
        "a0": pltpu.VMEM((group, 24, 128), F32),
        "a1": pltpu.VMEM((group, stat_y, 128), F32),
        "b1": pltpu.VMEM((n_y, stat_y, 128), F32),
        "a2": pltpu.VMEM((group, stat_z, 128), F32),
        "b2": pltpu.VMEM((n_y, stat_z, 128), F32),
        "c2": pltpu.VMEM((n_z, stat_z, 128), F32),
        "local": dma((2,)),
        "perm_s": dma((3,)),
        "perm_r": dma((3,)),
        "x_s": dma((2, n_x)),
        "x_r": dma((2, n_x)),
        "out_s": dma((n_x,)),
        "out_r": dma((n_x,)),
        "err_s": dma((n_x,)),
        "err_r": dma((n_x,)),
        "core_s": dma((2,)),
        "core_r": dma((2,)),
        "y_s": dma((2, n_y)),
        "y_r": dma((2, n_y)),
        "z_s": dma((n_z,)),
        "z_r": dma((n_z,)),
        "a0_s": dma((group,)),
        "a0_r": dma((group,)),
        "a1_s": dma((group,)),
        "a1_r": dma((group,)),
        "b1_s": dma((n_y,)),
        "b1_r": dma((n_y,)),
        "a2_s": dma((group,)),
        "a2_r": dma((group,)),
        "b2_s": dma((n_y,)),
        "b2_r": dma((n_y,)),
        "c2_s": dma((n_z,)),
        "c2_r": dma((n_z,)),
    }


class Refs:
    pass


def kernel(n_x, n_y, names, x_hbm, target_hbm, w_in_hbm, w_out_hbm, first_out, second_out, *scratch):
    s = Refs()
    for name, ref in zip(names, scratch):
        setattr(s, name, ref)
    n_z = 2 * n_y
    rows, width = x_hbm.shape
    hidden = w_in_hbm.shape[1]
    quarter = rows // n_x
    half, part, own = width // 2, width // (2 * n_y), width // (2 * n_y * n_z)
    width_tile, hidden_tile = tile_of(width), tile_of(hidden)

    me = lax.axis_index("dp")
    x = lax.axis_index("tensor")
    c = lax.rem(me, 2)
    y = lax.rem(lax.div(me, 2), n_y)
    z = lax.div(me, 2 * n_y)

    def dev(z_, y_, c_, x_):
        return {"dp": (z_ * n_y + y_) * 2 + c_, "tensor": x_}

    target_dev = dev(c * n_y + y, lax.rem(lax.rem(z, n_y) + y, n_y), 1 - lax.div(z, n_y), x)
    from_core = lax.div(z, n_y)
    from_y = lax.rem(z, n_y)
    y_node = lax.rem(y - from_y + n_y, n_y)
    source_dev = dev((1 - c) * n_y + y_node, from_y, from_core, x)
    z_node = from_y * 2 + from_core

    def x_peer(k):
        return dev(z, y, c, lax.rem(x + k, n_x))

    def group_peer(k):
        return dev(z, y, lax.rem(c + k // n_x, 2), lax.rem(x + k % n_x, n_x))

    def y_peer(k):
        return dev(z, lax.rem(y + k, n_y), c, x)

    def z_peer(k):
        return dev(lax.rem(z + k, n_z), y, c, x)

    fetch_in = pltpu.make_async_copy(w_in_hbm, s.w_in, s.local.at[0])
    fetch_out = pltpu.make_async_copy(w_out_hbm, s.w_out, s.local.at[1])
    fetch_in.start()
    fetch_out.start()

    barrier = pltpu.get_barrier_semaphore()
    everyone = [target_dev, source_dev]
    everyone += [group_peer(k) for k in range(1, 2 * n_x)]
    everyone += [y_peer(k) for k in range(1, n_y)]
    everyone += [z_peer(k) for k in range(1, n_z)]
    for peer in everyone:
        pl.semaphore_signal(barrier, inc=1, device_id=peer, device_id_type=MESH)
    pl.semaphore_wait(barrier, len(everyone))

    sent = []

    def push(src, dst, send_sem, recv_sem, peer):
        copy = pltpu.make_async_remote_copy(
            src_ref=src,
            dst_ref=dst,
            send_sem=send_sem,
            recv_sem=recv_sem,
            device_id=peer,
            device_id_type=MESH,
        )
        copy.start()
        sent.append(copy)
        return copy

    cut = -(-quarter // 32) * 16
    pieces = [(0, cut), (cut, quarter - cut)]
    moved = []
    for p, (start, size) in enumerate(pieces):
        at = block(x * quarter + start, size, 16)
        moved.append(push(x_hbm.at[at], s.x.at[at], s.perm_s.at[p], s.perm_r.at[p], target_dev))
    moved.append(
        push(
            target_hbm.at[block(x * quarter, quarter, 16)],
            s.target,
            s.perm_s.at[2],
            s.perm_r.at[2],
            target_dev,
        )
    )

    order_rows = tile_of(width)

    @pl.loop(0, width // order_rows)
    def _(step):
        base = step * order_rows
        i = lax.broadcasted_iota(jnp.int32, (order_rows, 128), 0) + base
        core_part = (i >= half).astype(jnp.int32)
        i = i - core_part * half
        y_part = jnp.zeros_like(i)
        for k in range(1, n_y):
            y_part = y_part + (i >= k * part).astype(jnp.int32)
        i = i - y_part * part
        z_part = jnp.zeros_like(i)
        for k in range(1, n_z):
            z_part = z_part + (i >= k * own).astype(jnp.int32)
        i = i - z_part * own
        column = ((z_part * n_y + y_part) * 2 + core_part) * own + i
        lanes = lax.broadcasted_iota(jnp.int32, (order_rows, 128), 1)
        for j in range(0, width, 128):
            size = min(128, width - j)
            hot = jnp.where(column == lanes + j, 1.0, 0.0)
            s.order[block(base, order_rows, 16), j : j + size] = hot[:, :size].astype(BF16)

    gathered = [{}, {}]
    for p, (start, size) in enumerate(pieces):
        moved[p].wait_recv()
        at = block(x * quarter + start, size, 16)
        for k in range(1, n_x):
            gathered[p][k] = push(
                s.x.at[at], s.x.at[at], s.x_s.at[p, k], s.x_r.at[p, k], x_peer(k)
            )

    fetch_in.wait()
    fetch_out.wait()

    steps = [0] + sorted(range(1, n_x), key=lambda k: min(k, n_x - k))
    partials = {}
    for k in steps:
        r = lax.rem(x - k + n_x, n_x)
        at = block(r * quarter, quarter, 16)
        if k:
            for p in range(2):
                gathered[p][k].wait_recv()

        @pl.loop(0, hidden // hidden_tile)
        def _(j):
            cols = block(j * hidden_tile, hidden_tile, hidden_tile)
            v = jnp.dot(s.x[at, :], s.w_in[:, cols], preferred_element_type=F32)
            v2 = v * v
            t = jnp.tanh(GELU_A * (v + GELU_B * (v * v2)))
            s.hid[at, cols] = (0.5 * v * (1.0 + t)).astype(BF16)
            s.slope[at, cols] = 0.5 * (1.0 + t) + (0.5 * v) * (1.0 - t * t) * (
                GELU_A * (1.0 + (3.0 * GELU_B) * v2)
            )

        @pl.loop(0, width // width_tile)
        def _(j):
            cols = block(j * width_tile, width_tile, width_tile)
            o = jnp.dot(s.hid[at, :], s.w_out[:, cols], preferred_element_type=F32)
            if k == 0:
                s.out_own[:, cols] = o
            else:
                s.out_send[k - 1, :, cols] = o.astype(BF16)

        if k:
            partials[k] = push(
                s.out_send.at[k - 1],
                s.out_recv.at[k - 1],
                s.out_s.at[k],
                s.out_r.at[k],
                dev(z, y, c, r),
            )

    @pl.loop(0, width // order_rows)
    def _(step):
        at = block(step * order_rows, order_rows, 16)
        s.x_t[at, :] = lax.dot_general(
            s.order[at, :], s.x[...], BY_ROWS, preferred_element_type=F32
        ).astype(BF16)

    moved[2].wait_recv()
    for k in steps[1:]:
        partials[k].wait_recv()

    @pl.loop(0, quarter // 16)
    def _(i):
        at = block(i * 16, 16, 16)
        total = s.out_own[at, :]
        for k in range(1, n_x):
            total = total + s.out_recv[k - 1, at, :].astype(F32)
        error = (total - s.target[at, :].astype(F32)) / rows
        s.err[block(x * quarter + i * 16, 16, 16), :] = error.astype(BF16)

    errors = {}
    mine = block(x * quarter, quarter, 16)
    for k in range(1, n_x):
        errors[k] = push(
            s.err.at[mine], s.err.at[mine], s.err_s.at[k], s.err_r.at[k], x_peer(k)
        )
    for k in steps:
        r = lax.rem(x - k + n_x, n_x)
        at = block(r * quarter, quarter, 16)
        if k:
            errors[k].wait_recv()

        @pl.loop(0, hidden // hidden_tile)
        def _(j):
            cols = block(j * hidden_tile, hidden_tile, hidden_tile)
            back = lax.dot_general(
                s.err[at, :], s.w_out[cols, :], BY_ROWS, preferred_element_type=F32
            )
            s.dpre[at, cols] = (back * s.slope[at, cols]).astype(BF16)

    mine = block(c * half, half, 16)
    theirs = block((1 - c) * half, half, 16)
    partner = dev(z, y, 1 - c, x)
    crossed = []
    for m, (left, right) in enumerate(((s.x_t, s.dpre), (s.err_t, s.hid))):
        if m == 1:

            @pl.loop(0, width // order_rows)
            def _(step):
                at = block(step * order_rows, order_rows, 16)
                s.err_t[at, :] = lax.dot_general(
                    s.order[at, :], s.err[...], BY_ROWS, preferred_element_type=F32
                ).astype(BF16)

        @pl.loop(0, hidden // hidden_tile)
        def _(j):
            cols = block(j * hidden_tile, hidden_tile, hidden_tile)
            s.send[m, :, cols] = jnp.dot(
                left[theirs, :], right[:, cols], preferred_element_type=F32
            ).astype(BF16)

        crossed.append(push(s.send.at[m], s.recv.at[m], s.core_s.at[m], s.core_r.at[m], partner))

        @pl.loop(0, hidden // hidden_tile)
        def _(j):
            cols = block(j * hidden_tile, hidden_tile, hidden_tile)
            s.keep[m, :, cols] = jnp.dot(
                left[mine, :], right[:, cols], preferred_element_type=F32
            )

    def total_over(buffer, send_sem, recv_sem, peer_of, count):
        copies = [
            push(buffer.at[0], buffer.at[k], send_sem.at[k], recv_sem.at[k], peer_of(k))
            for k in range(1, count)
        ]
        for copy in copies:
            copy.wait_recv()
        total = buffer[0]
        for k in range(1, count):
            total = total + buffer[k]
        return total

    stats = (jnp.zeros((8, 128), F32),) * 3
    for m in range(2):
        crossed[m].wait_recv()

        def level_sums(i, carry):
            at = block(i * 16, 16, 16)
            a = s.keep[m, at, :]
            b = s.recv[m, at, :].astype(F32)
            return (carry[0] + fold(a * b), carry[1] + fold(a * a), carry[2] + fold(b * b))

        stats = lax.fori_loop(0, half // 16, level_sums, stats)
    is_low = c == 1
    s.a0[0, 0:8, :] = stats[0]
    s.a0[0, 8:16, :] = jnp.where(is_low, stats[1], stats[2])
    s.a0[0, 16:24, :] = jnp.where(is_low, stats[2], stats[1])
    total = total_over(s.a0, s.a0_s, s.a0_r, group_peer, 2 * n_x)
    product, norm_low, norm_high = (
        jnp.sum(total[i * 8 : i * 8 + 8], keepdims=True) for i in range(3)
    )
    weights = tree_weights({(0, 0): norm_low, (0, 1): product, (1, 1): norm_high}, 2)
    weight_own = jnp.where(is_low, weights[0], weights[1])
    weight_other = jnp.where(is_low, weights[1], weights[0])

    y_copies = []
    for k in list(range(1, n_y)) + [0]:
        part_at = lax.rem(y + k, n_y) * part

        @pl.loop(0, part // 16)
        def _(i):
            at = block(part_at + i * 16, 16, 16)
            for m in range(2):
                node = weight_own * s.keep[m, at, :] + weight_other * s.recv[m, at, :].astype(F32)
                node = node.astype(BF16)
                if k:
                    s.node[m, at, :] = node
                else:
                    s.y_recv[y_node, m, block(i * 16, 16, 16), :] = node

        if k:
            for m in range(2):
                y_copies.append(
                    push(
                        s.node.at[m, block(part_at, part, 16)],
                        s.y_recv.at[y_node, m],
                        s.y_s.at[m, k],
                        s.y_r.at[m, k],
                        y_peer(k),
                    )
                )
    for copy in y_copies:
        copy.wait_recv()

    y_pairs = pairs_of(n_y)

    def y_sums(i, carry):
        at = block(i * 16, 16, 16)
        for m in range(2):
            nodes = [s.y_recv[j, m, at, :].astype(F32) for j in range(n_y)]
            carry = tuple(
                old + fold(nodes[a] * nodes[b]) for old, (a, b) in zip(carry, y_pairs)
            )
        return carry

    stats = lax.fori_loop(0, part // 16, y_sums, (jnp.zeros((8, 128), F32),) * len(y_pairs))
    s.a1[0] = jnp.zeros(s.a1.shape[1:], F32)
    for i, value in enumerate(stats):
        s.a1[0, i : i + 1, :] = jnp.sum(value, axis=0, keepdims=True)
    s.b1[0] = total_over(s.a1, s.a1_s, s.a1_r, group_peer, 2 * n_x)
    total = total_over(s.b1, s.b1_s, s.b1_r, y_peer, n_y)
    total = jnp.sum(total, axis=1, keepdims=True)
    weights = tree_weights({pair: total[i : i + 1] for i, pair in enumerate(y_pairs)}, n_y)

    @pl.loop(0, part // 16)
    def _(i):
        at = block(i * 16, 16, 16)
        for m in range(2):
            merged = weights[0] * s.y_recv[0, m, at, :].astype(F32)
            for j in range(1, n_y):
                merged = merged + weights[j] * s.y_recv[j, m, at, :].astype(F32)
            s.y_merged[m, at, :] = merged

    for j in range(n_z):
        for m in range(2):
            s.z_send[j, m] = s.y_merged[m, j * own : (j + 1) * own, :].astype(BF16)

    z_copies = []
    for k in range(1, n_z):
        z_copies.append(
            push(
                s.z_send.at[lax.rem(z + k, n_z)],
                s.z_recv.at[z_node],
                s.z_s.at[k],
                s.z_r.at[k],
                z_peer(k),
            )
        )
    s.z_recv[z_node] = s.z_send[z]
    for copy in z_copies:
        copy.wait_recv()

    z_pairs = pairs_of(n_z)
    s.a2[0] = jnp.zeros(s.a2.shape[1:], F32)
    for i, (a, b) in enumerate(z_pairs):
        value = 0.0
        for m in range(2):
            value = value + s.z_recv[a, m].astype(F32) * s.z_recv[b, m].astype(F32)
        s.a2[0, i : i + 1, :] = fold_row(value)
    s.b2[0] = total_over(s.a2, s.a2_s, s.a2_r, group_peer, 2 * n_x)
    s.c2[0] = total_over(s.b2, s.b2_s, s.b2_r, y_peer, n_y)
    total = total_over(s.c2, s.c2_s, s.c2_r, z_peer, n_z)
    total = jnp.sum(total, axis=1, keepdims=True)
    weights = tree_weights({pair: total[i : i + 1] for i, pair in enumerate(z_pairs)}, n_z)
    for m, out in enumerate((first_out, second_out)):
        merged = weights[0] * s.z_recv[0, m].astype(F32)
        for j in range(1, n_z):
            merged = merged + weights[j] * s.z_recv[j, m].astype(F32)
        out[...] = merged
    for copy in sent:
        copy.wait_send()


def solution(mesh):
    n_x = mesh.shape["tensor"]
    n_y = math.isqrt(mesh.shape["dp"] // 4)

    def on_device(inputs, targets, w_in, w_out):
        rows, width = inputs.shape
        hidden = w_in.shape[1]
        scratch = scratch_of(n_x, n_y, rows, width, hidden)
        share = jax.ShapeDtypeStruct((width // mesh.shape["dp"], hidden), F32)
        return pl.pallas_call(
            functools.partial(kernel, n_x, n_y, tuple(scratch)),
            out_shape=(share, share),
            in_specs=[pl.BlockSpec(memory_space=pl.ANY)] * 4,
            out_specs=(pl.BlockSpec(memory_space=pltpu.VMEM),) * 2,
            scratch_shapes=list(scratch.values()),
            compiler_params=pltpu.CompilerParams(
                collective_id=0, has_side_effects=True, vmem_limit_bytes=67_000_000
            ),
        )(inputs, targets, w_in, w_out)

    placed = (P("dp", None), P("dp", None), P(None, "tensor"), P("tensor", None))
    return jax.shard_map(
        on_device,
        mesh=mesh,
        in_specs=placed,
        out_specs=(P("dp", "tensor"), P("dp", "tensor")),
        check_vma=False,
    )
```

time: 787 us -> 213 us (0.27); the launches traced: 777 us -> 213 us
  waiting for transfers between devices: 497 us -> 0 us
  Pallas kernels: 0 us -> 209 us
  starting transfers between devices: 91.7 us -> 0 us
  between operations: 52.5 us -> 0.64 us
  other arithmetic: 51.3 us -> 0 us
  blocking collectives: 38.9 us -> 0 us
  matrix products: 25.4 us -> 0 us
  local copies, waits for them, and re-layouts: 20.9 us -> 3.12 us
    ppermute x33 -> x0, waiting for transfers between devices: 421 us -> none  [from_partner(): return lax.ppermute(value, axis, pairs)]
    pallas_call x0 -> x1, Pallas kernels: none -> 209 us  [on_device(): pl.pallas_call(functools.partial(kernel, n_x, n_y, tuple(scratch)), out_s...]
    ppermute x33 -> x0, starting transfers between devices: 86.9 us -> none  [from_partner(): return lax.ppermute(value, axis, pairs)]
    all_to_all x1 -> x0, waiting for transfers between devices: 40.5 us -> none  [sum_at_owner(): tiles = lax.all_to_all(cut_along(x, dim, count), axis, 0, 0, tiled=True)]
    all_to_all x6 -> x0, blocking collectives: 38.9 us -> none  [copy_for_each(): return lax.all_to_all(copies, axis, split_axis=0, concat_axis=0, tiled=True)]
    all_gather x1 -> x0, waiting for transfers between devices: 35 us -> none  [on_device(): error = lax.all_gather(error_share, 'tensor', axis=0, tiled=True)]
    reduce_sum x19 -> x0, other arithmetic: 29.5 us -> none  [the longest x12 26.1 us: combine(): product = jnp.sum(own[0] * incoming[0]) + jnp.sum(own[1] * incoming[1])]
    dot_general x4 -> x0, matrix products: 25.4 us -> none  [the longest x1 12.3 us: on_device(): lax.dot_general(inputs, dpre, contract_rows, preferred_element_type=jnp.f...]
  transfers between devices with their start and end apart: 35 -> 0, of which waited for: 33 -> 0; matrix products, arithmetic and copies ran while one was open for 3% -> 0% of each run, Pallas kernels for 0% -> 0%
where the time goes in v1:
time: 213 us
  Pallas kernels  209 us (98%)
  local copies, waits for them, and re-layouts  3.12 us (1%)
    pallas_call x1, Pallas kernels, on_device(): pl.pallas_call(functools.partial(kernel, n_x, n_y, tuple(scratch)), out_s...  209 us

profile of v1, /device:TPU:1, one launch (start us, length us, event | category | flops | bytes accessed | tf_op | source)
XLA Modules:
  0.0 212.7 jit_solution(3019843940109044987)
XLA Ops:
  0.6 208.9 %shard_map.59 = (f32[20,1280]{1,0:T(8,128)}, f32[20,1280]{1,0:T(8,128)}) custom-call(bf16[704,1280]{1,0:T(8,128)(2,1)} %x_hbm.1, bf16[704,1280]{1,0:T(8,128)(2,1)} %target_hbm.1, bf16[1280,1280]{1,0:T(8,128)(2,1)} %w_in_hbm.1, bf16[1280,1280]{1,0:T(8,128)(2,1)} %w_out_hbm.1), custom_call_target="tpu_custom_call" | custom-call | tf_op jit(solution)/shard_map/pallas_call | solution.py:517
  209.6 1.6 copy.8
  211.1 1.6 copy.9

commit v2 on v1

--- a/solution.py
+++ b/solution.py
@@ -41,6 +41,14 @@
     for j in range(128, v.shape[1], 128):
         s = s + t[:, j : j + 128]
     return s
+
+
+def pieces_of(rows):
+    units, pieces = rows // 16, []
+    for p in range(4):
+        start = p * units // 4
+        pieces.append((start * 16, ((p + 1) * units // 4 - start) * 16))
+    return pieces
 
 
 def pairs_of(n):
@@ -89,7 +97,7 @@
         "target": pltpu.VMEM((quarter, width), BF16),
         "order": pltpu.VMEM((width, width), BF16),
         "x_t": pltpu.VMEM((width, rows), BF16),
-        "err_t": pltpu.VMEM((width, rows), BF16),
+        "err_t": pltpu.VMEM((n_x, width, quarter), BF16),
         "hid": pltpu.VMEM((rows, hidden), BF16),
         "slope": pltpu.VMEM((rows, hidden), F32),
         "out_own": pltpu.VMEM((quarter, width), F32),
@@ -97,7 +105,8 @@
         "out_recv": pltpu.VMEM((n_x - 1, quarter, width), BF16),
         "err": pltpu.VMEM((rows, width), BF16),
         "dpre": pltpu.VMEM((rows, hidden), BF16),
-        "keep": pltpu.VMEM((2, half, hidden), F32),
+        "keep": pltpu.VMEM((half, hidden), F32),
+        "second": pltpu.VMEM((width, hidden), F32),
         "send": pltpu.VMEM((2, half, hidden), BF16),
         "recv": pltpu.VMEM((2, half, hidden), BF16),
         "node": pltpu.VMEM((2, half, hidden), BF16),
@@ -112,14 +121,18 @@
         "b2": pltpu.VMEM((n_y, stat_z, 128), F32),
         "c2": pltpu.VMEM((n_z, stat_z, 128), F32),
         "local": dma((2,)),
-        "perm_s": dma((3,)),
-        "perm_r": dma((3,)),
-        "x_s": dma((2, n_x)),
-        "x_r": dma((2, n_x)),
+        "relay": pltpu.VMEM((quarter, width), BF16),
+        "target_relay": pltpu.VMEM((quarter, width), BF16),
+        "hop1_s": dma((5,)),
+        "hop1_r": dma((5,)),
+        "hop2_s": dma((5,)),
+        "hop2_r": dma((5,)),
+        "x_s": dma((4, n_x)),
+        "x_r": dma((4, n_x)),
         "out_s": dma((n_x,)),
         "out_r": dma((n_x,)),
-        "err_s": dma((n_x,)),
-        "err_r": dma((n_x,)),
+        "err_s": dma((4, n_x)),
+        "err_r": dma((4, n_x)),
         "core_s": dma((2,)),
         "core_r": dma((2,)),
         "y_s": dma((2, n_y)),
@@ -165,11 +178,15 @@
     def dev(z_, y_, c_, x_):
         return {"dp": (z_ * n_y + y_) * 2 + c_, "tensor": x_}
 
-    target_dev = dev(c * n_y + y, lax.rem(lax.rem(z, n_y) + y, n_y), 1 - lax.div(z, n_y), x)
+    z_low = lax.rem(z, n_y)
+    relay_dev = dev(z, lax.rem(y + z_low, n_y), 1 - c, x)
+    relayed_y = lax.rem(y - z_low + n_y, n_y)
+    relayed_dev = dev(z, relayed_y, 1 - c, x)
+    final_dev = dev((1 - c) * n_y + relayed_y, y, lax.div(z, n_y), x)
     from_core = lax.div(z, n_y)
     from_y = lax.rem(z, n_y)
     y_node = lax.rem(y - from_y + n_y, n_y)
-    source_dev = dev((1 - c) * n_y + y_node, from_y, from_core, x)
+    source_dev = dev(c * n_y + y_node, y, 1 - from_core, x)
     z_node = from_y * 2 + from_core
 
     def x_peer(k):
@@ -190,7 +207,7 @@
     fetch_out.start()
 
     barrier = pltpu.get_barrier_semaphore()
-    everyone = [target_dev, source_dev]
+    everyone = [relay_dev, relayed_dev, final_dev, source_dev]
     everyone += [group_peer(k) for k in range(1, 2 * n_x)]
     everyone += [y_peer(k) for k in range(1, n_y)]
     everyone += [z_peer(k) for k in range(1, n_z)]
@@ -213,21 +230,122 @@
         sent.append(copy)
         return copy
 
-    cut = -(-quarter // 32) * 16
-    pieces = [(0, cut), (cut, quarter - cut)]
+    pieces = pieces_of(quarter)
+    share = block(x * quarter, quarter, 16)
+    x_from, target_from = x_hbm.at[share], target_hbm.at[share]
+    hops = []
+    for p, (start, size) in enumerate(pieces):
+        at = pl.ds(start, size)
+        hops.append(
+            push(x_from.at[at], s.relay.at[at], s.hop1_s.at[p], s.hop1_r.at[p], relay_dev)
+        )
     moved = []
     for p, (start, size) in enumerate(pieces):
-        at = block(x * quarter + start, size, 16)
-        moved.append(push(x_hbm.at[at], s.x.at[at], s.perm_s.at[p], s.perm_r.at[p], target_dev))
-    moved.append(
+        hops[p].wait_recv()
+        moved.append(
+            push(
+                s.relay.at[pl.ds(start, size)],
+                s.x.at[block(x * quarter + start, size, 16)],
+                s.hop2_s.at[p],
+                s.hop2_r.at[p],
+                final_dev,
+            )
+        )
+    last_piece = len(pieces)
+    hops.append(
         push(
-            target_hbm.at[block(x * quarter, quarter, 16)],
-            s.target,
-            s.perm_s.at[2],
-            s.perm_r.at[2],
-            target_dev,
+            target_from,
+            s.target_relay,
+            s.hop1_s.at[last_piece],
+            s.hop1_r.at[last_piece],
+            relay_dev,
         )
     )
+
+    near = sorted({1, n_x - 1})
+    relays = [(p, near[p * len(near) // len(pieces)]) for p in (0, 2, 1, 3)]
+
+    def rows_of(k, p):
+        start, size = pieces[p]
+        return block(lax.rem(x - k + n_x, n_x) * quarter + start, size, 16)
+
+    def give(ref, p, send_sem, recv_sem):
+        at = rows_of(0, p)
+        return {
+            (k, p): push(ref.at[at], ref.at[at], send_sem.at[p, k], recv_sem.at[p, k], x_peer(k))
+            for k in near
+        }
+
+    def relay(ref, given, send_sem, recv_sem):
+        if n_x == 4:
+            for p, k in relays:
+                given[(k, p)].wait_recv()
+                at = rows_of(k, p)
+                given[(2, p)] = push(
+                    ref.at[at], ref.at[at], send_sem.at[p, 2], recv_sem.at[p, 2], x_peer(k)
+                )
+
+    def take(given, k):
+        for p in range(len(pieces)):
+            if n_x < 4 or (p, k) not in relays:
+                given[(k, p)].wait_recv()
+
+    given = {}
+    for p in range(len(pieces)):
+        moved[p].wait_recv()
+        given.update(give(s.x, p, s.x_s, s.x_r))
+
+    fetch_in.wait()
+    fetch_out.wait()
+
+    steps = [0] + sorted(range(1, n_x), key=lambda k: min(k, n_x - k))
+    partials = {}
+    for k in steps:
+        r = lax.rem(x - k + n_x, n_x)
+        at = block(r * quarter, quarter, 16)
+        if k == 1:
+            relay(s.x, given, s.x_s, s.x_r)
+            hops[last_piece].wait_recv()
+            moved.append(
+                push(
+                    s.target_relay,
+                    s.target,
+                    s.hop2_s.at[last_piece],
+                    s.hop2_r.at[last_piece],
+                    final_dev,
+                )
+            )
+        if k:
+            take(given, k)
+
+        @pl.loop(0, hidden // hidden_tile)
+        def _(j):
+            cols = block(j * hidden_tile, hidden_tile, hidden_tile)
+            v = jnp.dot(s.x[at, :], s.w_in[:, cols], preferred_element_type=F32)
+            v2 = v * v
+            t = jnp.tanh(GELU_A * (v + GELU_B * (v * v2)))
+            s.hid[at, cols] = (0.5 * v * (1.0 + t)).astype(BF16)
+            s.slope[at, cols] = 0.5 * (1.0 + t) + (0.5 * v) * (1.0 - t * t) * (
+                GELU_A * (1.0 + (3.0 * GELU_B) * v2)
+            )
+
+        @pl.loop(0, width // width_tile)
+        def _(j):
+            cols = block(j * width_tile, width_tile, width_tile)
+            o = jnp.dot(s.hid[at, :], s.w_out[:, cols], preferred_element_type=F32)
+            if k == 0:
+                s.out_own[:, cols] = o
+            else:
+                s.out_send[k - 1, :, cols] = o.astype(BF16)
+
+        if k:
+            partials[k] = push(
+                s.out_send.at[k - 1],
+                s.out_recv.at[k - 1],
+                s.out_s.at[k],
+                s.out_r.at[k],
+                dev(z, y, c, r),
+            )
 
     order_rows = tile_of(width)
 
@@ -252,56 +370,6 @@
             hot = jnp.where(column == lanes + j, 1.0, 0.0)
             s.order[block(base, order_rows, 16), j : j + size] = hot[:, :size].astype(BF16)
 
-    gathered = [{}, {}]
-    for p, (start, size) in enumerate(pieces):
-        moved[p].wait_recv()
-        at = block(x * quarter + start, size, 16)
-        for k in range(1, n_x):
-            gathered[p][k] = push(
-                s.x.at[at], s.x.at[at], s.x_s.at[p, k], s.x_r.at[p, k], x_peer(k)
-            )
-
-    fetch_in.wait()
-    fetch_out.wait()
-
-    steps = [0] + sorted(range(1, n_x), key=lambda k: min(k, n_x - k))
-    partials = {}
-    for k in steps:
-        r = lax.rem(x - k + n_x, n_x)
-        at = block(r * quarter, quarter, 16)
-        if k:
-            for p in range(2):
-                gathered[p][k].wait_recv()
-
-        @pl.loop(0, hidden // hidden_tile)
-        def _(j):
-            cols = block(j * hidden_tile, hidden_tile, hidden_tile)
-            v = jnp.dot(s.x[at, :], s.w_in[:, cols], preferred_element_type=F32)
-            v2 = v * v
-            t = jnp.tanh(GELU_A * (v + GELU_B * (v * v2)))
-            s.hid[at, cols] = (0.5 * v * (1.0 + t)).astype(BF16)
-            s.slope[at, cols] = 0.5 * (1.0 + t) + (0.5 * v) * (1.0 - t * t) * (
-                GELU_A * (1.0 + (3.0 * GELU_B) * v2)
-            )
-
-        @pl.loop(0, width // width_tile)
-        def _(j):
-            cols = block(j * width_tile, width_tile, width_tile)
-            o = jnp.dot(s.hid[at, :], s.w_out[:, cols], preferred_element_type=F32)
-            if k == 0:
-                s.out_own[:, cols] = o
-            else:
-                s.out_send[k - 1, :, cols] = o.astype(BF16)
-
-        if k:
-            partials[k] = push(
-                s.out_send.at[k - 1],
-                s.out_recv.at[k - 1],
-                s.out_s.at[k],
-                s.out_r.at[k],
-                dev(z, y, c, r),
-            )
-
     @pl.loop(0, width // order_rows)
     def _(step):
         at = block(step * order_rows, order_rows, 16)
@@ -309,7 +377,7 @@
             s.order[at, :], s.x[...], BY_ROWS, preferred_element_type=F32
         ).astype(BF16)
 
-    moved[2].wait_recv()
+    moved[last_piece].wait_recv()
     for k in steps[1:]:
         partials[k].wait_recv()
 
@@ -322,17 +390,36 @@
         error = (total - s.target[at, :].astype(F32)) / rows
         s.err[block(x * quarter + i * 16, 16, 16), :] = error.astype(BF16)
 
-    errors = {}
-    mine = block(x * quarter, quarter, 16)
-    for k in range(1, n_x):
-        errors[k] = push(
-            s.err.at[mine], s.err.at[mine], s.err_s.at[k], s.err_r.at[k], x_peer(k)
-        )
-    for k in steps:
+    given = {}
+    for p in range(len(pieces)):
+        given.update(give(s.err, p, s.err_s, s.err_r))
+    mine = block(c * half, half, 16)
+    theirs = block((1 - c) * half, half, 16)
+    partner = dev(z, y, 1 - c, x)
+    crossed = []
+
+    def cross(m):
+        crossed.append(push(s.send.at[m], s.recv.at[m], s.core_s.at[m], s.core_r.at[m], partner))
+
+    def gradient_first(at, store):
+        @pl.loop(0, hidden // hidden_tile)
+        def _(j):
+            cols = block(j * hidden_tile, hidden_tile, hidden_tile)
+            store(cols, jnp.dot(s.x_t[at, :], s.dpre[:, cols], preferred_element_type=F32))
+
+    def store_send(cols, value):
+        s.send[0, :, cols] = value.astype(BF16)
+
+    def store_keep(cols, value):
+        s.keep[:, cols] = value
+
+    for turn, k in enumerate(steps):
         r = lax.rem(x - k + n_x, n_x)
         at = block(r * quarter, quarter, 16)
+        if k == 1:
+            relay(s.err, given, s.err_s, s.err_r)
         if k:
-            errors[k].wait_recv()
+            take(given, k)
 
         @pl.loop(0, hidden // hidden_tile)
         def _(j):
@@ -342,35 +429,44 @@
             )
             s.dpre[at, cols] = (back * s.slope[at, cols]).astype(BF16)
 
-    mine = block(c * half, half, 16)
-    theirs = block((1 - c) * half, half, 16)
-    partner = dev(z, y, 1 - c, x)
-    crossed = []
-    for m, (left, right) in enumerate(((s.x_t, s.dpre), (s.err_t, s.hid))):
-        if m == 1:
-
-            @pl.loop(0, width // order_rows)
-            def _(step):
-                at = block(step * order_rows, order_rows, 16)
-                s.err_t[at, :] = lax.dot_general(
-                    s.order[at, :], s.err[...], BY_ROWS, preferred_element_type=F32
-                ).astype(BF16)
+        last = turn == len(steps) - 1
+        if last:
+            gradient_first(theirs, store_send)
+            cross(0)
+
+        @pl.loop(0, width // order_rows)
+        def _(step):
+            some = block(step * order_rows, order_rows, 16)
+            s.err_t[k, some, :] = lax.dot_general(
+                s.order[some, :], s.err[at, :], BY_ROWS, preferred_element_type=F32
+            ).astype(BF16)
 
         @pl.loop(0, hidden // hidden_tile)
         def _(j):
             cols = block(j * hidden_tile, hidden_tile, hidden_tile)
-            s.send[m, :, cols] = jnp.dot(
-                left[theirs, :], right[:, cols], preferred_element_type=F32
-            ).astype(BF16)
-
-        crossed.append(push(s.send.at[m], s.recv.at[m], s.core_s.at[m], s.core_r.at[m], partner))
-
-        @pl.loop(0, hidden // hidden_tile)
-        def _(j):
-            cols = block(j * hidden_tile, hidden_tile, hidden_tile)
-            s.keep[m, :, cols] = jnp.dot(
-                left[mine, :], right[:, cols], preferred_element_type=F32
-            )
+            if last:
+                s.send[1, :, cols] = (
+                    s.second[theirs, cols]
+                    + jnp.dot(s.err_t[k, theirs, :], s.hid[at, cols], preferred_element_type=F32)
+                ).astype(BF16)
+                s.second[mine, cols] += jnp.dot(
+                    s.err_t[k, mine, :], s.hid[at, cols], preferred_element_type=F32
+                )
+            else:
+                value = jnp.dot(s.err_t[k], s.hid[at, cols], preferred_element_type=F32)
+                if turn == 0:
+                    s.second[:, cols] = value
+                else:
+                    s.second[:, cols] += value
+
+        if last:
+            cross(1)
+            gradient_first(mine, store_keep)
+
+    def own_part(m, start):
+        if m == 0:
+            return s.keep[block(start, 16, 16), :]
+        return s.second[block(c * half + start, 16, 16), :]
 
     def total_over(buffer, send_sem, recv_sem, peer_of, count):
         copies = [
@@ -390,12 +486,12 @@
 
         def level_sums(i, carry):
             at = block(i * 16, 16, 16)
-            a = s.keep[m, at, :]
+            a = own_part(m, i * 16)
             b = s.recv[m, at, :].astype(F32)
             return (carry[0] + fold(a * b), carry[1] + fold(a * a), carry[2] + fold(b * b))
 
         stats = lax.fori_loop(0, half // 16, level_sums, stats)
-    is_low = c == 1
+    is_low = c == 0
     s.a0[0, 0:8, :] = stats[0]
     s.a0[0, 8:16, :] = jnp.where(is_low, stats[1], stats[2])
     s.a0[0, 16:24, :] = jnp.where(is_low, stats[2], stats[1])
@@ -415,7 +511,8 @@
         def _(i):
             at = block(part_at + i * 16, 16, 16)
             for m in range(2):
-                node = weight_own * s.keep[m, at, :] + weight_other * s.recv[m, at, :].astype(F32)
+                node = weight_own * own_part(m, part_at + i * 16)
+                node = node + weight_other * s.recv[m, at, :].astype(F32)
                 node = node.astype(BF16)
                 if k:
                     s.node[m, at, :] = node

time: 213 us -> 194 us (0.911)
  Pallas kernels: 209 us -> 190 us
    pallas_call x1, Pallas kernels: 209 us -> 190 us  [on_device(): pl.pallas_call(functools.partial(kernel, n_x, n_y, tuple(scratch)), out_s...]
where the time goes in v2:
time: 194 us
  Pallas kernels  190 us (98%)
  local copies, waits for them, and re-layouts  3.12 us (2%)
    pallas_call x1, Pallas kernels, on_device(): pl.pallas_call(functools.partial(kernel, n_x, n_y, tuple(scratch)), out_s...  190 us

profile of v2, /device:TPU:1, one launch (start us, length us, event | category | flops | bytes accessed | tf_op | source)
XLA Modules:
  0.0 194.0 jit_solution(14188605040769130113)
XLA Ops:
  0.6 190.2 %shard_map.59 = (f32[20,1280]{1,0:T(8,128)}, f32[20,1280]{1,0:T(8,128)}) custom-call(bf16[704,1280]{1,0:T(8,128)(2,1)} %x_hbm.1, bf16[704,1280]{1,0:T(8,128)(2,1)} %target_hbm.1, bf16[1280,1280]{1,0:T(8,128)(2,1)} %w_in_hbm.1, bf16[1280,1280]{1,0:T(8,128)(2,1)} %w_out_hbm.1), custom_call_target="tpu_custom_call" | custom-call | tf_op jit(solution)/shard_map/pallas_call | solution.py:614
  190.8 1.6 copy.8
  192.4 1.6 copy.9

commit v3 on v2

--- a/solution.py
+++ b/solution.py
@@ -49,6 +49,26 @@
         start = p * units // 4
         pieces.append((start * 16, ((p + 1) * units // 4 - start) * 16))
     return pieces
+
+
+def diagonal(n):
+    shape = (n, 128)
+    return lax.broadcasted_iota(jnp.int32, shape, 0) == lax.broadcasted_iota(jnp.int32, shape, 1)
+
+
+def pack(rows, values):
+    rows[...] = jnp.zeros(rows.shape, F32)
+    for i, value in enumerate(values):
+        rows[i : i + 1, :] = jnp.sum(value, axis=0, keepdims=True)
+    column = jnp.sum(rows[...], axis=1, keepdims=True)
+    line = jnp.sum(jnp.where(diagonal(rows.shape[0]), column, 0.0), axis=0, keepdims=True)
+    return jnp.broadcast_to(line, (8, 128))
+
+
+def unpack(total, names, n):
+    line = jnp.broadcast_to(total[0:1], (n, 128))
+    column = jnp.sum(jnp.where(diagonal(n), line, 0.0), axis=1, keepdims=True)
+    return {name: column[i : i + 1] for i, name in enumerate(names)}
 
 
 def pairs_of(n):
@@ -89,10 +109,13 @@
     stat_y = -(-len(pairs_of(n_y)) // 8) * 8
     stat_z = -(-len(pairs_of(n_z)) // 8) * 8
     group = 2 * n_x
+    tiles = width // tile_of(width)
     dma = pltpu.SemaphoreType.DMA
     return {
         "w_in": pltpu.VMEM((width, hidden), BF16),
         "w_out": pltpu.VMEM((hidden, width), BF16),
+        "w_back": pltpu.VMEM((hidden, width), BF16),
+        "target_back": pltpu.VMEM((quarter, width), BF16),
         "x": pltpu.VMEM((rows, width), BF16),
         "target": pltpu.VMEM((quarter, width), BF16),
         "order": pltpu.VMEM((width, width), BF16),
@@ -101,8 +124,8 @@
         "hid": pltpu.VMEM((rows, hidden), BF16),
         "slope": pltpu.VMEM((rows, hidden), F32),
         "out_own": pltpu.VMEM((quarter, width), F32),
-        "out_send": pltpu.VMEM((n_x - 1, quarter, width), BF16),
-        "out_recv": pltpu.VMEM((n_x - 1, quarter, width), BF16),
+        "out_send": pltpu.VMEM((n_x - 1, tiles, quarter, width // tiles), BF16),
+        "out_recv": pltpu.VMEM((n_x - 1, tiles, quarter, width // tiles), BF16),
         "err": pltpu.VMEM((rows, width), BF16),
         "dpre": pltpu.VMEM((rows, hidden), BF16),
         "keep": pltpu.VMEM((half, hidden), F32),
@@ -114,12 +137,15 @@
         "y_merged": pltpu.VMEM((2, part, hidden), F32),
         "z_send": pltpu.VMEM((n_z, 2, own, hidden), BF16),
         "z_recv": pltpu.VMEM((n_z, 2, own, hidden), BF16),
-        "a0": pltpu.VMEM((group, 24, 128), F32),
-        "a1": pltpu.VMEM((group, stat_y, 128), F32),
-        "b1": pltpu.VMEM((n_y, stat_y, 128), F32),
-        "a2": pltpu.VMEM((group, stat_z, 128), F32),
-        "b2": pltpu.VMEM((n_y, stat_z, 128), F32),
-        "c2": pltpu.VMEM((n_z, stat_z, 128), F32),
+        "r0": pltpu.VMEM((8, 128), F32),
+        "r1": pltpu.VMEM((stat_y, 128), F32),
+        "r2": pltpu.VMEM((stat_z, 128), F32),
+        "a0": pltpu.VMEM((group, 8, 128), F32),
+        "a1": pltpu.VMEM((group, 8, 128), F32),
+        "b1": pltpu.VMEM((n_y, 8, 128), F32),
+        "a2": pltpu.VMEM((group, 8, 128), F32),
+        "b2": pltpu.VMEM((n_y, 8, 128), F32),
+        "c2": pltpu.VMEM((n_z, 8, 128), F32),
         "local": dma((2,)),
         "relay": pltpu.VMEM((quarter, width), BF16),
         "target_relay": pltpu.VMEM((quarter, width), BF16),
@@ -129,8 +155,8 @@
         "hop2_r": dma((5,)),
         "x_s": dma((4, n_x)),
         "x_r": dma((4, n_x)),
-        "out_s": dma((n_x,)),
-        "out_r": dma((n_x,)),
+        "out_s": dma((tiles, n_x)),
+        "out_r": dma((tiles, n_x)),
         "err_s": dma((4, n_x)),
         "err_r": dma((4, n_x)),
         "core_s": dma((2,)),
@@ -239,6 +265,29 @@
         hops.append(
             push(x_from.at[at], s.relay.at[at], s.hop1_s.at[p], s.hop1_r.at[p], relay_dev)
         )
+    order_rows = tile_of(width)
+
+    @pl.loop(0, width // order_rows)
+    def _(step):
+        base = step * order_rows
+        i = lax.broadcasted_iota(jnp.int32, (order_rows, 128), 0) + base
+        core_part = (i >= half).astype(jnp.int32)
+        i = i - core_part * half
+        y_part = jnp.zeros_like(i)
+        for k in range(1, n_y):
+            y_part = y_part + (i >= k * part).astype(jnp.int32)
+        i = i - y_part * part
+        z_part = jnp.zeros_like(i)
+        for k in range(1, n_z):
+            z_part = z_part + (i >= k * own).astype(jnp.int32)
+        i = i - z_part * own
+        column = ((z_part * n_y + y_part) * 2 + core_part) * own + i
+        lanes = lax.broadcasted_iota(jnp.int32, (order_rows, 128), 1)
+        for j in range(0, width, 128):
+            size = min(128, width - j)
+            hot = jnp.where(column == lanes + j, 1.0, 0.0)
+            s.order[block(base, order_rows, 16), j : j + size] = hot[:, :size].astype(BF16)
+
     moved = []
     for p, (start, size) in enumerate(pieces):
         hops[p].wait_recv()
@@ -262,6 +311,14 @@
         )
     )
 
+    fetch_out.wait()
+
+    def reorder_w(t):
+        cols = pl.ds(t * width_tile, width_tile)
+        s.w_back[:, cols] = lax.dot_general(
+            s.w_out[...], s.order[cols, :], BY_ROWS, preferred_element_type=F32
+        ).astype(BF16)
+
     near = sorted({1, n_x - 1})
     relays = [(p, near[p * len(near) // len(pieces)]) for p in (0, 2, 1, 3)]
 
@@ -294,12 +351,15 @@
     for p in range(len(pieces)):
         moved[p].wait_recv()
         given.update(give(s.x, p, s.x_s, s.x_r))
+        if p < width // width_tile:
+            reorder_w(p)
+    for t in range(len(pieces), width // width_tile):
+        reorder_w(t)
 
     fetch_in.wait()
-    fetch_out.wait()
 
     steps = [0] + sorted(range(1, n_x), key=lambda k: min(k, n_x - k))
-    partials = {}
+    partials = []
     for k in steps:
         r = lax.rem(x - k + n_x, n_x)
         at = block(r * quarter, quarter, 16)
@@ -329,46 +389,22 @@
                 GELU_A * (1.0 + (3.0 * GELU_B) * v2)
             )
 
-        @pl.loop(0, width // width_tile)
-        def _(j):
-            cols = block(j * width_tile, width_tile, width_tile)
-            o = jnp.dot(s.hid[at, :], s.w_out[:, cols], preferred_element_type=F32)
+        for t in range(width // width_tile):
+            cols = pl.ds(t * width_tile, width_tile)
+            o = jnp.dot(s.hid[at, :], s.w_back[:, cols], preferred_element_type=F32)
             if k == 0:
                 s.out_own[:, cols] = o
             else:
-                s.out_send[k - 1, :, cols] = o.astype(BF16)
-
-        if k:
-            partials[k] = push(
-                s.out_send.at[k - 1],
-                s.out_recv.at[k - 1],
-                s.out_s.at[k],
-                s.out_r.at[k],
-                dev(z, y, c, r),
-            )
-
-    order_rows = tile_of(width)
-
-    @pl.loop(0, width // order_rows)
-    def _(step):
-        base = step * order_rows
-        i = lax.broadcasted_iota(jnp.int32, (order_rows, 128), 0) + base
-        core_part = (i >= half).astype(jnp.int32)
-        i = i - core_part * half
-        y_part = jnp.zeros_like(i)
-        for k in range(1, n_y):
-            y_part = y_part + (i >= k * part).astype(jnp.int32)
-        i = i - y_part * part
-        z_part = jnp.zeros_like(i)
-        for k in range(1, n_z):
-            z_part = z_part + (i >= k * own).astype(jnp.int32)
-        i = i - z_part * own
-        column = ((z_part * n_y + y_part) * 2 + core_part) * own + i
-        lanes = lax.broadcasted_iota(jnp.int32, (order_rows, 128), 1)
-        for j in range(0, width, 128):
-            size = min(128, width - j)
-            hot = jnp.where(column == lanes + j, 1.0, 0.0)
-            s.order[block(base, order_rows, 16), j : j + size] = hot[:, :size].astype(BF16)
+                s.out_send[k - 1, t] = o.astype(BF16)
+                partials.append(
+                    push(
+                        s.out_send.at[k - 1, t],
+                        s.out_recv.at[k - 1, t],
+                        s.out_s.at[t, k],
+                        s.out_r.at[t, k],
+                        dev(z, y, c, r),
+                    )
+                )
 
     @pl.loop(0, width // order_rows)
     def _(step):
@@ -378,17 +414,27 @@
         ).astype(BF16)
 
     moved[last_piece].wait_recv()
-    for k in steps[1:]:
-        partials[k].wait_recv()
+
+    @pl.loop(0, width // width_tile)
+    def _(j):
+        cols = block(j * width_tile, width_tile, width_tile)
+        s.target_back[:, cols] = lax.dot_general(
+            s.target[...], s.order[cols, :], BY_ROWS, preferred_element_type=F32
+        ).astype(BF16)
+
+    for copy in partials:
+        copy.wait_recv()
 
     @pl.loop(0, quarter // 16)
     def _(i):
         at = block(i * 16, 16, 16)
-        total = s.out_own[at, :]
-        for k in range(1, n_x):
-            total = total + s.out_recv[k - 1, at, :].astype(F32)
-        error = (total - s.target[at, :].astype(F32)) / rows
-        s.err[block(x * quarter + i * 16, 16, 16), :] = error.astype(BF16)
+        for t in range(width // width_tile):
+            cols = pl.ds(t * width_tile, width_tile)
+            total = s.out_own[at, cols]
+            for k in range(1, n_x):
+                total = total + s.out_recv[k - 1, t, at, :].astype(F32)
+            error = (total - s.target_back[at, cols].astype(F32)) / rows
+            s.err[block(x * quarter + i * 16, 16, 16), cols] = error.astype(BF16)
 
     given = {}
     for p in range(len(pieces)):
@@ -425,7 +471,7 @@
         def _(j):
             cols = block(j * hidden_tile, hidden_tile, hidden_tile)
             back = lax.dot_general(
-                s.err[at, :], s.w_out[cols, :], BY_ROWS, preferred_element_type=F32
+                s.err[at, :], s.w_back[cols, :], BY_ROWS, preferred_element_type=F32
             )
             s.dpre[at, cols] = (back * s.slope[at, cols]).astype(BF16)
 
@@ -434,12 +480,9 @@
             gradient_first(theirs, store_send)
             cross(0)
 
-        @pl.loop(0, width // order_rows)
-        def _(step):
-            some = block(step * order_rows, order_rows, 16)
-            s.err_t[k, some, :] = lax.dot_general(
-                s.order[some, :], s.err[at, :], BY_ROWS, preferred_element_type=F32
-            ).astype(BF16)
+        for t in range(width // width_tile):
+            cols = pl.ds(t * width_tile, width_tile)
+            s.err_t[k, cols, :] = s.err[at, cols].T
 
         @pl.loop(0, hidden // hidden_tile)
         def _(j):
@@ -492,36 +535,36 @@
 
         stats = lax.fori_loop(0, half // 16, level_sums, stats)
     is_low = c == 0
-    s.a0[0, 0:8, :] = stats[0]
-    s.a0[0, 8:16, :] = jnp.where(is_low, stats[1], stats[2])
-    s.a0[0, 16:24, :] = jnp.where(is_low, stats[2], stats[1])
+    s.a0[0] = pack(
+        s.r0,
+        (
+            stats[0],
+            jnp.where(is_low, stats[1], stats[2]),
+            jnp.where(is_low, stats[2], stats[1]),
+        ),
+    )
     total = total_over(s.a0, s.a0_s, s.a0_r, group_peer, 2 * n_x)
-    product, norm_low, norm_high = (
-        jnp.sum(total[i * 8 : i * 8 + 8], keepdims=True) for i in range(3)
-    )
-    weights = tree_weights({(0, 0): norm_low, (0, 1): product, (1, 1): norm_high}, 2)
+    weights = tree_weights(unpack(total, ((0, 1), (0, 0), (1, 1)), 8), 2)
     weight_own = jnp.where(is_low, weights[0], weights[1])
     weight_other = jnp.where(is_low, weights[1], weights[0])
 
-    y_copies = []
-    for k in list(range(1, n_y)) + [0]:
-        part_at = lax.rem(y + k, n_y) * part
-
-        @pl.loop(0, part // 16)
-        def _(i):
-            at = block(part_at + i * 16, 16, 16)
-            for m in range(2):
+    y_copies = [[], []]
+    for m in range(2):
+        for k in list(range(1, n_y)) + [0]:
+            part_at = lax.rem(y + k, n_y) * part
+
+            @pl.loop(0, part // 16)
+            def _(i):
+                at = block(part_at + i * 16, 16, 16)
                 node = weight_own * own_part(m, part_at + i * 16)
-                node = node + weight_other * s.recv[m, at, :].astype(F32)
-                node = node.astype(BF16)
+                node = (node + weight_other * s.recv[m, at, :].astype(F32)).astype(BF16)
                 if k:
                     s.node[m, at, :] = node
                 else:
                     s.y_recv[y_node, m, block(i * 16, 16, 16), :] = node
 
-        if k:
-            for m in range(2):
-                y_copies.append(
+            if k:
+                y_copies[m].append(
                     push(
                         s.node.at[m, block(part_at, part, 16)],
                         s.y_recv.at[y_node, m],
@@ -530,28 +573,24 @@
                         y_peer(k),
                     )
                 )
-    for copy in y_copies:
-        copy.wait_recv()
 
     y_pairs = pairs_of(n_y)
 
-    def y_sums(i, carry):
-        at = block(i * 16, 16, 16)
-        for m in range(2):
+    stats = (jnp.zeros((8, 128), F32),) * len(y_pairs)
+    for m in range(2):
+        for copy in y_copies[m]:
+            copy.wait_recv()
+
+        def y_sums(i, carry):
+            at = block(i * 16, 16, 16)
             nodes = [s.y_recv[j, m, at, :].astype(F32) for j in range(n_y)]
-            carry = tuple(
-                old + fold(nodes[a] * nodes[b]) for old, (a, b) in zip(carry, y_pairs)
-            )
-        return carry
-
-    stats = lax.fori_loop(0, part // 16, y_sums, (jnp.zeros((8, 128), F32),) * len(y_pairs))
-    s.a1[0] = jnp.zeros(s.a1.shape[1:], F32)
-    for i, value in enumerate(stats):
-        s.a1[0, i : i + 1, :] = jnp.sum(value, axis=0, keepdims=True)
+            return tuple(old + fold(nodes[a] * nodes[b]) for old, (a, b) in zip(carry, y_pairs))
+
+        stats = lax.fori_loop(0, part // 16, y_sums, stats)
+    s.a1[0] = pack(s.r1, stats)
     s.b1[0] = total_over(s.a1, s.a1_s, s.a1_r, group_peer, 2 * n_x)
     total = total_over(s.b1, s.b1_s, s.b1_r, y_peer, n_y)
-    total = jnp.sum(total, axis=1, keepdims=True)
-    weights = tree_weights({pair: total[i : i + 1] for i, pair in enumerate(y_pairs)}, n_y)
+    weights = tree_weights(unpack(total, y_pairs, s.r1.shape[0]), n_y)
 
     @pl.loop(0, part // 16)
     def _(i):
@@ -582,17 +621,17 @@
         copy.wait_recv()
 
     z_pairs = pairs_of(n_z)
-    s.a2[0] = jnp.zeros(s.a2.shape[1:], F32)
-    for i, (a, b) in enumerate(z_pairs):
+    stats = []
+    for a, b in z_pairs:
         value = 0.0
         for m in range(2):
             value = value + s.z_recv[a, m].astype(F32) * s.z_recv[b, m].astype(F32)
-        s.a2[0, i : i + 1, :] = fold_row(value)
+        stats.append(fold_row(value))
+    s.a2[0] = pack(s.r2, stats)
     s.b2[0] = total_over(s.a2, s.a2_s, s.a2_r, group_peer, 2 * n_x)
     s.c2[0] = total_over(s.b2, s.b2_s, s.b2_r, y_peer, n_y)
     total = total_over(s.c2, s.c2_s, s.c2_r, z_peer, n_z)
-    total = jnp.sum(total, axis=1, keepdims=True)
-    weights = tree_weights({pair: total[i : i + 1] for i, pair in enumerate(z_pairs)}, n_z)
+    weights = tree_weights(unpack(total, z_pairs, s.r2.shape[0]), n_z)
     for m, out in enumerate((first_out, second_out)):
         merged = weights[0] * s.z_recv[0, m].astype(F32)
         for j in range(1, n_z):

time: 194 us -> 187 us (0.964)
  Pallas kernels: 190 us -> 183 us
    pallas_call x1, Pallas kernels: 190 us -> 183 us  [on_device(): pl.pallas_call(functools.partial(kernel, n_x, n_y, tuple(scratch)), out_s...]
where the time goes in v3:
time: 187 us
  Pallas kernels  183 us (98%)
  local copies, waits for them, and re-layouts  3.12 us (2%)
    pallas_call x1, Pallas kernels, on_device(): pl.pallas_call(functools.partial(kernel, n_x, n_y, tuple(scratch)), out_s...  183 us

profile of v3, /device:TPU:1, one launch (start us, length us, event | category | flops | bytes accessed | tf_op | source)
XLA Modules:
  0.0 186.7 jit_solution(16073941829035984607)
XLA Ops:
  0.6 182.9 %shard_map.59 = (f32[20,1280]{1,0:T(8,128)}, f32[20,1280]{1,0:T(8,128)}) custom-call(bf16[704,1280]{1,0:T(8,128)(2,1)} %x_hbm.1, bf16[704,1280]{1,0:T(8,128)(2,1)} %target_hbm.1, bf16[1280,1280]{1,0:T(8,128)(2,1)} %w_in_hbm.1, bf16[1280,1280]{1,0:T(8,128)(2,1)} %w_out_hbm.1), custom_call_target="tpu_custom_call" | custom-call | tf_op jit(solution)/shard_map/pallas_call | solution.py:653
  183.5 1.6 copy.8
  185.1 1.6 copy.9

commit v4 on v3

--- a/solution.py
+++ b/solution.py
@@ -49,6 +49,10 @@
         start = p * units // 4
         pieces.append((start * 16, ((p + 1) * units // 4 - start) * 16))
     return pieces
+
+
+def groups_of(n_x):
+    return [[0], [1, 3], [2]] if n_x == 4 else [[k] for k in range(n_x)]
 
 
 def diagonal(n):
@@ -108,7 +112,7 @@
     half, part, own = width // 2, width // (2 * n_y), width // (2 * n_y * n_z)
     stat_y = -(-len(pairs_of(n_y)) // 8) * 8
     stat_z = -(-len(pairs_of(n_z)) // 8) * 8
-    group = 2 * n_x
+    everyone = 2 * n_x
     tiles = width // tile_of(width)
     dma = pltpu.SemaphoreType.DMA
     return {
@@ -120,7 +124,10 @@
         "target": pltpu.VMEM((quarter, width), BF16),
         "order": pltpu.VMEM((width, width), BF16),
         "x_t": pltpu.VMEM((width, rows), BF16),
-        "err_t": pltpu.VMEM((n_x, width, quarter), BF16),
+        **{
+            f"err_t{i}": pltpu.VMEM((width, len(group) * quarter), BF16)
+            for i, group in enumerate(groups_of(n_x))
+        },
         "hid": pltpu.VMEM((rows, hidden), BF16),
         "slope": pltpu.VMEM((rows, hidden), F32),
         "out_own": pltpu.VMEM((quarter, width), F32),
@@ -140,10 +147,10 @@
         "r0": pltpu.VMEM((8, 128), F32),
         "r1": pltpu.VMEM((stat_y, 128), F32),
         "r2": pltpu.VMEM((stat_z, 128), F32),
-        "a0": pltpu.VMEM((group, 8, 128), F32),
-        "a1": pltpu.VMEM((group, 8, 128), F32),
+        "a0": pltpu.VMEM((everyone, 8, 128), F32),
+        "a1": pltpu.VMEM((everyone, 8, 128), F32),
         "b1": pltpu.VMEM((n_y, 8, 128), F32),
-        "a2": pltpu.VMEM((group, 8, 128), F32),
+        "a2": pltpu.VMEM((everyone, 8, 128), F32),
         "b2": pltpu.VMEM((n_y, 8, 128), F32),
         "c2": pltpu.VMEM((n_z, 8, 128), F32),
         "local": dma((2,)),
@@ -165,14 +172,14 @@
         "y_r": dma((2, n_y)),
         "z_s": dma((n_z,)),
         "z_r": dma((n_z,)),
-        "a0_s": dma((group,)),
-        "a0_r": dma((group,)),
-        "a1_s": dma((group,)),
-        "a1_r": dma((group,)),
+        "a0_s": dma((everyone,)),
+        "a0_r": dma((everyone,)),
+        "a1_s": dma((everyone,)),
+        "a1_r": dma((everyone,)),
         "b1_s": dma((n_y,)),
         "b1_r": dma((n_y,)),
-        "a2_s": dma((group,)),
-        "a2_r": dma((group,)),
+        "a2_s": dma((everyone,)),
+        "a2_r": dma((everyone,)),
         "b2_s": dma((n_y,)),
         "b2_r": dma((n_y,)),
         "c2_s": dma((n_z,)),
@@ -294,7 +301,7 @@
         moved.append(
             push(
                 s.relay.at[pl.ds(start, size)],
-                s.x.at[block(x * quarter + start, size, 16)],
+                s.x.at[pl.ds(start, size)],
                 s.hop2_s.at[p],
                 s.hop2_r.at[p],
                 final_dev,
@@ -320,16 +327,20 @@
         ).astype(BF16)
 
     near = sorted({1, n_x - 1})
+    groups = groups_of(n_x)
+    slot = {k: i for i, k in enumerate(k for group in groups for k in group)}
     relays = [(p, near[p * len(near) // len(pieces)]) for p in (0, 2, 1, 3)]
 
     def rows_of(k, p):
         start, size = pieces[p]
-        return block(lax.rem(x - k + n_x, n_x) * quarter + start, size, 16)
+        return pl.ds(slot[k] * quarter + start, size)
 
     def give(ref, p, send_sem, recv_sem):
         at = rows_of(0, p)
         return {
-            (k, p): push(ref.at[at], ref.at[at], send_sem.at[p, k], recv_sem.at[p, k], x_peer(k))
+            (k, p): push(
+                ref.at[at], ref.at[rows_of(k, p)], send_sem.at[p, k], recv_sem.at[p, k], x_peer(k)
+            )
             for k in near
         }
 
@@ -339,7 +350,11 @@
                 given[(k, p)].wait_recv()
                 at = rows_of(k, p)
                 given[(2, p)] = push(
-                    ref.at[at], ref.at[at], send_sem.at[p, 2], recv_sem.at[p, 2], x_peer(k)
+                    ref.at[at],
+                    ref.at[rows_of(2, p)],
+                    send_sem.at[p, 2],
+                    recv_sem.at[p, 2],
+                    x_peer(k),
                 )
 
     def take(given, k):
@@ -358,12 +373,10 @@
 
     fetch_in.wait()
 
-    steps = [0] + sorted(range(1, n_x), key=lambda k: min(k, n_x - k))
     partials = []
-    for k in steps:
-        r = lax.rem(x - k + n_x, n_x)
-        at = block(r * quarter, quarter, 16)
-        if k == 1:
+    for turn, group in enumerate(groups):
+        at = pl.ds(slot[group[0]] * quarter, len(group) * quarter)
+        if turn == 1:
             relay(s.x, given, s.x_s, s.x_r)
             hops[last_piece].wait_recv()
             moved.append(
@@ -375,8 +388,9 @@
                     final_dev,
                 )
             )
-        if k:
-            take(given, k)
+        for k in group:
+            if k:
+                take(given, k)
 
         @pl.loop(0, hidden // hidden_tile)
         def _(j):
@@ -392,17 +406,18 @@
         for t in range(width // width_tile):
             cols = pl.ds(t * width_tile, width_tile)
             o = jnp.dot(s.hid[at, :], s.w_back[:, cols], preferred_element_type=F32)
-            if k == 0:
-                s.out_own[:, cols] = o
-            else:
-                s.out_send[k - 1, t] = o.astype(BF16)
+            for i, k in enumerate(group):
+                if k == 0:
+                    s.out_own[:, cols] = o
+                    continue
+                s.out_send[k - 1, t] = o[i * quarter : (i + 1) * quarter].astype(BF16)
                 partials.append(
                     push(
                         s.out_send.at[k - 1, t],
                         s.out_recv.at[k - 1, t],
                         s.out_s.at[t, k],
                         s.out_r.at[t, k],
-                        dev(z, y, c, r),
+                        x_peer(n_x - k),
                     )
                 )
 
@@ -434,7 +449,7 @@
             for k in range(1, n_x):
                 total = total + s.out_recv[k - 1, t, at, :].astype(F32)
             error = (total - s.target_back[at, cols].astype(F32)) / rows
-            s.err[block(x * quarter + i * 16, 16, 16), cols] = error.astype(BF16)
+            s.err[at, cols] = error.astype(BF16)
 
     given = {}
     for p in range(len(pieces)):
@@ -459,13 +474,14 @@
     def store_keep(cols, value):
         s.keep[:, cols] = value
 
-    for turn, k in enumerate(steps):
-        r = lax.rem(x - k + n_x, n_x)
-        at = block(r * quarter, quarter, 16)
-        if k == 1:
+    for turn, group in enumerate(groups):
+        at = pl.ds(slot[group[0]] * quarter, len(group) * quarter)
+        err_t = getattr(s, f"err_t{turn}")
+        if turn == 1:
             relay(s.err, given, s.err_s, s.err_r)
-        if k:
-            take(given, k)
+        for k in group:
+            if k:
+                take(given, k)
 
         @pl.loop(0, hidden // hidden_tile)
         def _(j):
@@ -475,14 +491,14 @@
             )
             s.dpre[at, cols] = (back * s.slope[at, cols]).astype(BF16)
 
-        last = turn == len(steps) - 1
+        last = turn == len(groups) - 1
         if last:
             gradient_first(theirs, store_send)
             cross(0)
 
         for t in range(width // width_tile):
             cols = pl.ds(t * width_tile, width_tile)
-            s.err_t[k, cols, :] = s.err[at, cols].T
+            err_t[cols, :] = s.err[at, cols].T
 
         @pl.loop(0, hidden // hidden_tile)
         def _(j):
@@ -490,13 +506,13 @@
             if last:
                 s.send[1, :, cols] = (
                     s.second[theirs, cols]
-                    + jnp.dot(s.err_t[k, theirs, :], s.hid[at, cols], preferred_element_type=F32)
+                    + jnp.dot(err_t[theirs, :], s.hid[at, cols], preferred_element_type=F32)
                 ).astype(BF16)
                 s.second[mine, cols] += jnp.dot(
-                    s.err_t[k, mine, :], s.hid[at, cols], preferred_element_type=F32
+                    err_t[mine, :], s.hid[at, cols], preferred_element_type=F32
                 )
             else:
-                value = jnp.dot(s.err_t[k], s.hid[at, cols], preferred_element_type=F32)
+                value = jnp.dot(err_t[...], s.hid[at, cols], preferred_element_type=F32)
                 if turn == 0:
                     s.second[:, cols] = value
                 else:

time: 187 us -> 183 us (0.979)
  Pallas kernels: 183 us -> 179 us
    pallas_call x1, Pallas kernels: 183 us -> 179 us  [on_device(): pl.pallas_call(functools.partial(kernel, n_x, n_y, tuple(scratch)), out_s...]
where the time goes in v4:
time: 183 us
  Pallas kernels  179 us (98%)
  local copies, waits for them, and re-layouts  3.12 us (2%)
    pallas_call x1, Pallas kernels, on_device(): pl.pallas_call(functools.partial(kernel, n_x, n_y, tuple(scratch)), out_s...  179 us

profile of v4, /device:TPU:1, one launch (start us, length us, event | category | flops | bytes accessed | tf_op | source)
XLA Modules:
  0.0 182.6 jit_solution(580146426835471326)
XLA Ops:
  0.6 178.8 %shard_map.59 = (f32[20,1280]{1,0:T(8,128)}, f32[20,1280]{1,0:T(8,128)}) custom-call(bf16[704,1280]{1,0:T(8,128)(2,1)} %x_hbm.1, bf16[704,1280]{1,0:T(8,128)(2,1)} %target_hbm.1, bf16[1280,1280]{1,0:T(8,128)(2,1)} %w_in_hbm.1, bf16[1280,1280]{1,0:T(8,128)(2,1)} %w_out_hbm.1), custom_call_target="tpu_custom_call" | custom-call | tf_op jit(solution)/shard_map/pallas_call | solution.py:669
  179.5 1.6 copy.8
  181.0 1.6 copy.9

commit v5 on v4

--- a/solution.py
+++ b/solution.py
@@ -112,7 +112,7 @@
     half, part, own = width // 2, width // (2 * n_y), width // (2 * n_y * n_z)
     stat_y = -(-len(pairs_of(n_y)) // 8) * 8
     stat_z = -(-len(pairs_of(n_z)) // 8) * 8
-    everyone = 2 * n_x
+    everyone, plane = 2 * n_x, 2 * n_x * n_y
     tiles = width // tile_of(width)
     dma = pltpu.SemaphoreType.DMA
     return {
@@ -148,10 +148,8 @@
         "r1": pltpu.VMEM((stat_y, 128), F32),
         "r2": pltpu.VMEM((stat_z, 128), F32),
         "a0": pltpu.VMEM((everyone, 8, 128), F32),
-        "a1": pltpu.VMEM((everyone, 8, 128), F32),
-        "b1": pltpu.VMEM((n_y, 8, 128), F32),
-        "a2": pltpu.VMEM((everyone, 8, 128), F32),
-        "b2": pltpu.VMEM((n_y, 8, 128), F32),
+        "a1": pltpu.VMEM((plane, 8, 128), F32),
+        "a2": pltpu.VMEM((plane, 8, 128), F32),
         "c2": pltpu.VMEM((n_z, 8, 128), F32),
         "local": dma((2,)),
         "relay": pltpu.VMEM((quarter, width), BF16),
@@ -174,14 +172,10 @@
         "z_r": dma((n_z,)),
         "a0_s": dma((everyone,)),
         "a0_r": dma((everyone,)),
-        "a1_s": dma((everyone,)),
-        "a1_r": dma((everyone,)),
-        "b1_s": dma((n_y,)),
-        "b1_r": dma((n_y,)),
-        "a2_s": dma((everyone,)),
-        "a2_r": dma((everyone,)),
-        "b2_s": dma((n_y,)),
-        "b2_r": dma((n_y,)),
+        "a1_s": dma((plane,)),
+        "a1_r": dma((plane,)),
+        "a2_s": dma((plane,)),
+        "a2_r": dma((plane,)),
         "c2_s": dma((n_z,)),
         "c2_r": dma((n_z,)),
     }
@@ -228,6 +222,15 @@
     def group_peer(k):
         return dev(z, y, lax.rem(c + k // n_x, 2), lax.rem(x + k % n_x, n_x))
 
+    def plane_peer(k):
+        group = k % (2 * n_x)
+        return dev(
+            z,
+            lax.rem(y + k // (2 * n_x), n_y),
+            lax.rem(c + group // n_x, 2),
+            lax.rem(x + group % n_x, n_x),
+        )
+
     def y_peer(k):
         return dev(z, lax.rem(y + k, n_y), c, x)
 
@@ -241,8 +244,7 @@
 
     barrier = pltpu.get_barrier_semaphore()
     everyone = [relay_dev, relayed_dev, final_dev, source_dev]
-    everyone += [group_peer(k) for k in range(1, 2 * n_x)]
-    everyone += [y_peer(k) for k in range(1, n_y)]
+    everyone += [plane_peer(k) for k in range(1, 2 * n_x * n_y)]
     everyone += [z_peer(k) for k in range(1, n_z)]
     for peer in everyone:
         pl.semaphore_signal(barrier, inc=1, device_id=peer, device_id_type=MESH)
@@ -604,8 +606,7 @@
 
         stats = lax.fori_loop(0, part // 16, y_sums, stats)
     s.a1[0] = pack(s.r1, stats)
-    s.b1[0] = total_over(s.a1, s.a1_s, s.a1_r, group_peer, 2 * n_x)
-    total = total_over(s.b1, s.b1_s, s.b1_r, y_peer, n_y)
+    total = total_over(s.a1, s.a1_s, s.a1_r, plane_peer, 2 * n_x * n_y)
     weights = tree_weights(unpack(total, y_pairs, s.r1.shape[0]), n_y)
 
     @pl.loop(0, part // 16)
@@ -644,8 +645,7 @@
             value = value + s.z_recv[a, m].astype(F32) * s.z_recv[b, m].astype(F32)
         stats.append(fold_row(value))
     s.a2[0] = pack(s.r2, stats)
-    s.b2[0] = total_over(s.a2, s.a2_s, s.a2_r, group_peer, 2 * n_x)
-    s.c2[0] = total_over(s.b2, s.b2_s, s.b2_r, y_peer, n_y)
+    s.c2[0] = total_over(s.a2, s.a2_s, s.a2_r, plane_peer, 2 * n_x * n_y)
     total = total_over(s.c2, s.c2_s, s.c2_r, z_peer, n_z)
     weights = tree_weights(unpack(total, z_pairs, s.r2.shape[0]), n_z)
     for m, out in enumerate((first_out, second_out)):

time: 183 us -> 181 us (0.989)
  Pallas kernels: 179 us -> 177 us
where the time goes in v5:
time: 181 us
  Pallas kernels  177 us (98%)
  local copies, waits for them, and re-layouts  3.12 us (2%)
    pallas_call x1, Pallas kernels, on_device(): pl.pallas_call(functools.partial(kernel, n_x, n_y, tuple(scratch)), out_s...  177 us

profile of v5, /device:TPU:1, one launch (start us, length us, event | category | flops | bytes accessed | tf_op | source)
XLA Modules:
  0.0 180.8 jit_solution(17374095834389336132)
XLA Ops:
  0.6 177.0 %shard_map.59 = (f32[20,1280]{1,0:T(8,128)}, f32[20,1280]{1,0:T(8,128)}) custom-call(bf16[704,1280]{1,0:T(8,128)(2,1)} %x_hbm.1, bf16[704,1280]{1,0:T(8,128)(2,1)} %target_hbm.1, bf16[1280,1280]{1,0:T(8,128)(2,1)} %w_in_hbm.1, bf16[1280,1280]{1,0:T(8,128)(2,1)} %w_out_hbm.1), custom_call_target="tpu_custom_call" | custom-call | tf_op jit(solution)/shard_map/pallas_call | solution.py:669
  177.7 1.6 copy.8
  179.2 1.6 copy.9
